TPU v7x, 32 devices: a whole 2x2x4 slice. The times are simulated.
32 devices in a mesh: mem: 4 (over z), gx: 4 (over y, core), gy: 2 (over x).
Axes of the slice: x: 2, y: 2, z: 4, core: 2. Of those that a mesh axis runs over, the one named last changes fastest.
Arguments:
- height: float32 [4, 4, 128, 256], P('mem', None, 'gx', 'gy'), may hold values from -4 to 4
- wind: float32 [4, 2, 4, 128, 256], P('mem', None, None, 'gx', 'gy'), may hold values from -0.8 to 0.8
- moisture: float32 [4, 4, 128, 256], P('mem', None, 'gx', 'gy'), may hold values from 0 to 2
- coeffs: float32 [4, 4, 4, 16384], P('mem', None, None, ('gx', 'gy')), may hold values from -6 to 6
- damping: float32 [16384], P(('gx', 'gy')), may hold values from 0.3 to 1
- vmix: float32 [4, 4], replicated, may hold values from -3 to 3
- basis: bfloat16 [16384, 384], P(('gx', 'gy')), may hold values from -0.046875 to 0.046875
- edge_source: int32 [768], replicated, may hold values from 0 to 383
- row_cell: int32 [128], replicated, may hold values from 0 to 15, never falling along the last dimension, each value on 1 to 16 neighbouring positions
- col_cell: int32 [256], replicated, may hold values from 0 to 31, never falling along the last dimension, each value on 1 to 16 neighbouring positions
- cond_rate: float32 [4], replicated, may hold values from 0.05 to 0.5
- saturation: float32 [4], replicated, may hold values from 0.5 to 1.5
- ancestry: int32 [4], replicated, may hold values from 0 to 3
Outputs:
- height_out: float32 [4, 4, 128, 256], P('mem', None, 'gx', 'gy')
- wind_out: float32 [4, 2, 4, 128, 256], P('mem', None, None, 'gx', 'gy')
- moisture_out: float32 [4, 4, 128, 256], P('mem', None, 'gx', 'gy')
- rainfall: float32 [4, 128, 256], P('mem', 'gx', 'gy')
- restricted: float32 [4, 4, 16, 32], P('mem')
- coeffs_out: float32 [4, 4, 4, 16384], P('mem', None, None, ('gx', 'gy'))
Inputs may be any that keep to these rules, and one draw needn't show every extreme that they name: row_cell never falls, and each of the 16 global rows holds 1 to 16 nest rows, one exactly 16. col_cell never falls, and each of the 32 global columns holds 1 to 16 nest columns, one exactly 16.
All inputs are finite; a program needn't handle non-finite values.
Results may differ from a plain program's by a relative error of at most 0.00035.
Values sent between devices are 32-bit elements; how exact they have to be, the bound alone decides.
A program may use at most 64 MiB of HBM per device.

v0:
```python
import jax
import jax.numpy as jnp
from jax import lax
from jax.sharding import PartitionSpec as P

RATIO = 8
ACOUSTIC = 2
acoustic_substep = 0.2
drift_step = 0.4


def extended(block, sides, width):
    for axis, dim in sides:
        count = lax.axis_size(axis)
        forward = [(i, i + 1) for i in range(count - 1)]
        backward = [(target, source) for source, target in forward]
        low = lax.ppermute(
            lax.slice_in_dim(block, block.shape[dim] - width, None, axis=dim), axis, forward
        )
        high = lax.ppermute(lax.slice_in_dim(block, 0, width, axis=dim), axis, backward)
        block = jnp.concatenate([low, block, high], axis=dim)
    return block


def side_values(rim, indices, rim_points, levels):
    table = (indices[None, :] == lax.iota(jnp.int32, rim_points)[:, None]).astype(jnp.float32)
    return jnp.dot(rim, table, precision=lax.Precision.HIGHEST).reshape(4, levels, indices.shape[0])


def frame(padded, sides, flags):
    western_edge, eastern_edge, southern_edge, northern_edge = sides
    at_west, at_east, at_south, at_north = flags
    size_x = padded.shape[2] - 2
    size_y = padded.shape[3] - 2
    current = padded[:, :, 0, 1 : 1 + size_y]
    padded = padded.at[:, :, 0, 1 : 1 + size_y].set(jnp.where(at_west, western_edge, current))
    current = padded[:, :, 1 + size_x, 1 : 1 + size_y]
    padded = padded.at[:, :, 1 + size_x, 1 : 1 + size_y].set(
        jnp.where(at_east, eastern_edge, current)
    )
    current = padded[:, :, 1 : 1 + size_x, 0]
    padded = padded.at[:, :, 1 : 1 + size_x, 0].set(jnp.where(at_south, southern_edge, current))
    current = padded[:, :, 1 : 1 + size_x, 1 + size_y]
    padded = padded.at[:, :, 1 : 1 + size_x, 1 + size_y].set(
        jnp.where(at_north, northern_edge, current)
    )
    return padded


def pick_sides(sides, first, last):
    return tuple((side[first:last] for side in sides))


def body(
    height,
    wind,
    moisture,
    coeffs,
    damping,
    vmix,
    basis,
    edge_source,
    row_cell,
    col_cell,
    cond_rate,
    saturation,
    ancestry,
):
    levels = height.shape[1]
    size_x = height.shape[2]
    size_y = height.shape[3]
    full_x = row_cell.shape[0]
    full_y = col_cell.shape[0]
    rim_points = basis.shape[1]
    row_index = lax.axis_index("gx")
    col_index = lax.axis_index("gy")
    row_start = row_index * size_x
    col_start = col_index * size_y
    coeff_new = jnp.einsum("lj,mfjk->mflk", vmix, coeffs, precision=lax.Precision.HIGHEST) * damping
    coeff_low = coeff_new.astype(jnp.bfloat16).reshape(4 * levels, -1)
    rim_part = jnp.dot(coeff_low, basis, preferred_element_type=jnp.float32)
    rim = lax.psum(rim_part, ("gx", "gy"))
    western_edge = side_values(
        rim, lax.dynamic_slice_in_dim(edge_source, col_start, size_y), rim_points, levels
    )
    eastern_edge = side_values(
        rim, lax.dynamic_slice_in_dim(edge_source, full_y + col_start, size_y), rim_points, levels
    )
    southern_edge = side_values(
        rim,
        lax.dynamic_slice_in_dim(edge_source, 2 * full_y + row_start, size_x),
        rim_points,
        levels,
    )
    northern_edge = side_values(
        rim,
        lax.dynamic_slice_in_dim(edge_source, 2 * full_y + full_x + row_start, size_x),
        rim_points,
        levels,
    )
    sides = (western_edge, eastern_edge, southern_edge, northern_edge)
    flags = (
        row_index == 0,
        row_index == lax.axis_size("gx") - 1,
        col_index == 0,
        col_index == lax.axis_size("gy") - 1,
    )
    h_field = height[0]
    u_field = wind[0, 0]
    v_field = wind[0, 1]
    q_field = moisture[0]
    for substep in range(ACOUSTIC):
        h_pad = extended(h_field[None], (("gx", 2), ("gy", 3)), 1)
        h_pad = frame(h_pad, pick_sides(sides, 0, 1), flags)[0]
        u_field = u_field - acoustic_substep * (h_pad[:, 2:, 1:-1] - h_pad[:, :-2, 1:-1])
        v_field = v_field - acoustic_substep * (h_pad[:, 1:-1, 2:] - h_pad[:, 1:-1, :-2])
        wind_pad = extended(jnp.stack([u_field, v_field]), (("gx", 2), ("gy", 3)), 1)
        wind_pad = frame(wind_pad, pick_sides(sides, 1, 3), flags)
        u_pad = wind_pad[0]
        v_pad = wind_pad[1]
        h_field = h_field - acoustic_substep * (
            u_pad[:, 2:, 1:-1] - u_pad[:, :-2, 1:-1] + (v_pad[:, 1:-1, 2:] - v_pad[:, 1:-1, :-2])
        )
    q_pad = extended(q_field[None], (("gx", 2), ("gy", 3)), 1)
    q_pad = frame(q_pad, pick_sides(sides, 3, 4), flags)[0]
    flux = (
        jnp.maximum(u_field, 0.0) * (q_field - q_pad[:, :-2, 1:-1])
        + jnp.minimum(u_field, 0.0) * (q_pad[:, 2:, 1:-1] - q_field)
        + (
            jnp.maximum(v_field, 0.0) * (q_field - q_pad[:, 1:-1, :-2])
            + jnp.minimum(v_field, 0.0) * (q_pad[:, 1:-1, 2:] - q_field)
        )
    )
    q_field = q_field - drift_step * flux
    excess = jnp.maximum(q_field - saturation[:, None, None], 0.0)
    fallen = cond_rate[:, None, None] * excess
    q_field = q_field - fallen
    rain = jnp.sum(fallen, axis=0)
    coarse_rows = full_x // RATIO
    coarse_cols = full_y // RATIO
    row_table = (row_cell[None, :] == lax.iota(jnp.int32, coarse_rows)[:, None]).astype(jnp.float32)
    col_table = (col_cell[None, :] == lax.iota(jnp.int32, coarse_cols)[:, None]).astype(jnp.float32)
    row_count = jnp.sum(row_table, axis=1)
    col_count = jnp.sum(col_table, axis=1)
    local_rows = lax.dynamic_slice_in_dim(row_table, row_start, size_x, 1)
    local_cols = lax.dynamic_slice_in_dim(col_table, col_start, size_y, 1)
    partial_value = jnp.einsum("ax,lxy->lay", local_rows, q_field, precision=lax.Precision.HIGHEST)
    partial_value = jnp.einsum(
        "lay,by->lab", partial_value, local_cols, precision=lax.Precision.HIGHEST
    )
    sums = lax.psum(partial_value, "gy")
    sums = lax.psum(sums, "gx")
    coarse = sums / (row_count[:, None] * col_count[None, :])
    states = (
        h_field[None],
        jnp.stack([u_field, v_field])[None],
        q_field[None],
        rain[None],
        coarse[None],
        coeff_new,
    )
    member_here = lax.axis_index("mem")
    everyone = (
        lax.all_gather(states[0], "mem", axis=0, tiled=True),
        lax.all_gather(states[1], "mem", axis=0, tiled=True),
        lax.all_gather(states[2], "mem", axis=0, tiled=True),
        lax.all_gather(states[3], "mem", axis=0, tiled=True),
        lax.all_gather(states[4], "mem", axis=0, tiled=True),
        lax.all_gather(states[5], "mem", axis=0, tiled=True),
    )
    source = ancestry[member_here]
    cloned = tuple(
        (lax.dynamic_index_in_dim(whole, source, 0, keepdims=True) for whole in everyone)
    )
    return (cloned[0], cloned[1], cloned[2], cloned[3], cloned[4], cloned[5])


def solution(mesh):
    in_specs = (
        P("mem", None, "gx", "gy"),
        P("mem", None, None, "gx", "gy"),
        P("mem", None, "gx", "gy"),
        P("mem", None, None, ("gx", "gy")),
        P(("gx", "gy")),
        P(),
        P(("gx", "gy"), None),
        P(),
        P(),
        P(),
        P(),
        P(),
        P(),
    )
    out_specs = (
        P("mem", None, "gx", "gy"),
        P("mem", None, None, "gx", "gy"),
        P("mem", None, "gx", "gy"),
        P("mem", "gx", "gy"),
        P("mem", None, None, None),
        P("mem", None, None, ("gx", "gy")),
    )
    return jax.shard_map(body, mesh=mesh, in_specs=in_specs, out_specs=out_specs, check_vma=False)
```

profile of v0, /device:TPU:10, one launch (start us, length us, event | category | flops | bytes accessed | tf_op | source)
XLA Modules:
  0.0 245.4 jit_solution(11485259475965265100)
XLA Ops:
  5.3 4.3 %collective-permute-start.16 = (f32[1,4,1,128]{3,1,2,0:T(4,128)S(1)}, f32[1,4,1,128]{3,1,2,0:T(4,128)S(1)}, u32[]{:S(2)}, u32[]{:S(2)}) collective-permute-start(f32[1,4,1,128]{3,1,2,0:T(4,128)S(1)} %copy.119), channel_id=1, source_target_pairs={{0,2},{2,4},{4,6},{1,3},{3,5},{5,7},{8,10},{10,12},{12,14},{9,11},... | collective-permute-start | bytes 6152 | tf_op jit(solution)/shard_map/ppermute | solution.py:17
  18.1 25.0 %psum.21 = f32[16,384]{1,0:T(8,128)S(1)} all-reduce(f32[16,384]{1,0:T(8,128)S(1)} %fusion.78), channel_id=1, replica_groups=mesh['mem'=4,'gx'=4,'gy'=2] {'gx','gy'}, use_global_device_ids=true, to_apply=%region_0.0 | all-reduce | flops 6144 | bytes 49152 | tf_op jit(solution)/shard_map/psum | solution.py:82
  44.0 16.5 %all_gather.23 = f32[4,4,4,2048]{3,2,1,0:T(4,128)S(1)} all-gather(f32[1,4,4,2048]{3,2,1,0:T(4,128)S(1)} %get-tuple-element.293), channel_id=1, replica_groups=mesh['mem'=4,'gx'=4,'gy'=2] {'mem'}, dimensions={0}, use_global_device_ids=true | all-gather | bytes 655360 | tf_op jit(solution)/shard_map/all_gather | solution.py:169
  63.0 3.3 %collective-permute-start.3 = (f32[1,4,34,1]{3,1,2,0:T(4,128)S(1)}, f32[1,4,34,1]{3,1,2,0:T(4,128)S(1)}, u32[]{:S(2)}, u32[]{:S(2)}) collective-permute-start(f32[1,4,34,1]{3,1,2,0:T(4,128)S(1)} %get-tuple-element.271), channel_id=1, source_target_pairs={{1,0},{3,2},{5,4},{7,6},{9,8},{11,10},{13,12},{15,14},{17,16},{19,... | collective-permute-start | bytes 1640 | tf_op jit(solution)/shard_map/ppermute | solution.py:20
  68.2 4.3 %collective-permute-done.2 = f32[1,4,34,1]{3,1,2,0:T(4,128)S(1)} collective-permute-done((f32[1,4,34,1]{3,1,2,0:T(4,128)S(1)}, f32[1,4,34,1]{3,1,2,0:T(4,128)S(1)}, u32[]{:S(2)}, u32[]{:S(2)}) %collective-permute-start.2) | collective-permute-done | bytes 576 | tf_op jit(solution)/shard_map/ppermute | solution.py:17
  75.2 2.4 scatter.71
  79.1 3.0 %collective-permute-start.4 = (f32[2,4,1,128]{3,1,2,0:T(4,128)S(1)}, f32[2,4,1,128]{3,1,2,0:T(4,128)S(1)}, u32[]{:S(2)}, u32[]{:S(2)}) collective-permute-start(f32[2,4,1,128]{3,1,2,0:T(4,128)S(1)} %get-tuple-element.262), channel_id=1, source_target_pairs={{0,2},{2,4},{4,6},{1,3},{3,5},{5,7},{8,10},{10,12},{12,14},{9,11},... | collective-permute-start | bytes 12296 | tf_op jit(solution)/shard_map/ppermute | solution.py:17
  85.4 4.6 %collective-permute-start.7 = (f32[2,4,34,1]{3,1,2,0:T(4,128)S(1)}, f32[2,4,34,1]{3,1,2,0:T(4,128)S(1)}, u32[]{:S(2)}, u32[]{:S(2)}) collective-permute-start(f32[2,4,34,1]{3,1,2,0:T(4,128)S(1)} %get-tuple-element.257), channel_id=1, source_target_pairs={{1,0},{3,2},{5,4},{7,6},{9,8},{11,10},{13,12},{15,14},{17,16},{19,... | collective-permute-start | bytes 3272 | tf_op jit(solution)/shard_map/ppermute | solution.py:20
  91.2 2.6 %collective-permute-done.7 = f32[2,4,34,1]{3,1,2,0:T(4,128)S(1)} collective-permute-done((f32[2,4,34,1]{3,1,2,0:T(4,128)S(1)}, f32[2,4,34,1]{3,1,2,0:T(4,128)S(1)}, u32[]{:S(2)}, u32[]{:S(2)}) %collective-permute-start.7) | collective-permute-done | bytes 1120 | tf_op jit(solution)/shard_map/ppermute | solution.py:20
  93.8 4.4 %collective-permute-done.6 = f32[2,4,34,1]{3,1,2,0:T(4,128)S(1)} collective-permute-done((f32[2,4,34,1]{3,1,2,0:T(4,128)S(1)}, f32[2,4,34,1]{3,1,2,0:T(4,128)S(1)}, u32[]{:S(2)}, u32[]{:S(2)}) %collective-permute-start.6) | collective-permute-done | bytes 1120 | tf_op jit(solution)/shard_map/ppermute | solution.py:17
  101.3 4.8 %scatter.79 = f32[2,4,34,130]{3,1,2,0:T(4,128)S(1)} dynamic-update-slice(f32[2,4,34,130]{3,1,2,0:T(4,128)S(1)} %scatter.76, f32[2,4,32,1]{3,1,2,0:T(4,128)S(1)} %slice_select_fusion.2, s32[]{:T(128)} %constant.509.clone.1, s32[]{:T(128)} %constant.509.clone.1, s32[]{:T(128)} %constant.516.clone.1, s32[]{:T(128)} %constant.522.clone.1) | dynamic-update-slice | bytes 2052 | tf_op jit(solution)/shard_map/scatter | solution.py:44
  116.0 3.4 %collective-permute-done.10 = f32[1,4,34,1]{3,1,2,0:T(4,128)S(1)} collective-permute-done((f32[1,4,34,1]{3,1,2,0:T(4,128)S(1)}, f32[1,4,34,1]{3,1,2,0:T(4,128)S(1)}, u32[]{:S(2)}, u32[]{:S(2)}) %collective-permute-start.10) | collective-permute-done | bytes 576 | tf_op jit(solution)/shard_map/ppermute | solution.py:17
  125.6 2.6 %scatter.85 = f32[4,34,130]{2,0,1:T(4,128)S(1)} dynamic-update-slice(f32[4,34,130]{2,0,1:T(4,128)S(1)} %bitcast.149, f32[4,32,1]{2,0,1:T(4,128)S(1)} %copy.88, s32[]{:T(128)} %constant.509.clone.1, s32[]{:T(128)} %constant.516.clone.1, s32[]{:T(128)} %constant.522.clone.1) | dynamic-update-slice | bytes 1028 | tf_op jit(solution)/shard_map/scatter | solution.py:44
  129.9 3.5 %collective-permute-start.12 = (f32[2,4,1,128]{3,1,2,0:T(4,128)S(1)}, f32[2,4,1,128]{3,1,2,0:T(4,128)S(1)}, u32[]{:S(2)}, u32[]{:S(2)}) collective-permute-start(f32[2,4,1,128]{3,1,2,0:T(4,128)S(1)} %get-tuple-element.260), channel_id=1, source_target_pairs={{0,2},{2,4},{4,6},{1,3},{3,5},{5,7},{8,10},{10,12},{12,14},{9,11},... | collective-permute-start | bytes 12296 | tf_op jit(solution)/shard_map/ppermute | solution.py:17
  133.4 16.1 %all-gather.1 = f32[8,4,32,128]{3,2,1,0:T(8,128)S(1)} all-gather(f32[2,4,32,128]{3,2,1,0:T(8,128)S(1)} %copy.92), channel_id=3, replica_groups=mesh['mem'=4,'gx'=4,'gy'=2] {'mem'}, dimensions={0}, use_global_device_ids=true | all-gather | bytes 655360 | tf_op jit(solution)/shard_map/all_gather | solution.py:165
  150.3 14.7 %all-gather.2 = f32[16,32,128]{2,1,0:T(8,128)S(1)} all-gather(f32[4,32,128]{2,1,0:T(8,128)S(1)} %copy.101), channel_id=4, replica_groups=mesh['mem'=4,'gx'=4,'gy'=2] {'mem'}, dimensions={0}, use_global_device_ids=true | all-gather | bytes 327680 | tf_op jit(solution)/shard_map/all_gather | solution.py:166
  165.7 13.2 %all-gather.3 = f32[128,128]{1,0:T(8,128)S(1)} all-gather(f32[32,128]{1,0:T(8,128)S(1)} %get-tuple-element.246), channel_id=5, replica_groups=mesh['mem'=4,'gx'=4,'gy'=2] {'mem'}, dimensions={0}, use_global_device_ids=true | all-gather | bytes 81920 | tf_op jit(solution)/shard_map/all_gather | solution.py:167
  179.2 7.0 %psum.22 = f32[4,16,32]{2,1,0:T(8,128)S(1)} all-reduce(f32[4,16,32]{2,1,0:T(8,128)S(1)} %fusion.36), channel_id=1, replica_groups=mesh['mem'=4,'gx'=4,'gy'=2] {'gy'}, use_global_device_ids=true, to_apply=%region_2.3 | all-reduce | flops 2048 | bytes 16384 | tf_op jit(solution)/shard_map/psum | solution.py:151
  186.2 10.3 %psum.23 = f32[4,16,32]{2,1,0:T(8,128)S(1)} all-reduce(f32[4,16,32]{2,1,0:T(8,128)S(1)} %psum.22), channel_id=1, replica_groups=mesh['mem'=4,'gx'=4,'gy'=2] {'gx'}, use_global_device_ids=true, to_apply=%region_3.4 | all-reduce | flops 2048 | bytes 16384 | tf_op jit(solution)/shard_map/psum | solution.py:152
  196.5 13.6 %all-gather.4 = f32[16,16,32]{2,1,0:T(8,128)S(1)} all-gather(f32[4,16,32]{2,1,0:T(8,128)S(1)} %broadcast_divide_fusion), channel_id=6, replica_groups=mesh['mem'=4,'gx'=4,'gy'=2] {'mem'}, dimensions={0}, use_global_device_ids=true | all-gather | bytes 40960 | tf_op jit(solution)/shard_map/all_gather | solution.py:168
  211.5 3.8 %collective-permute-start.15 = (f32[2,4,34,1]{3,1,2,0:T(4,128)S(1)}, f32[2,4,34,1]{3,1,2,0:T(4,128)S(1)}, u32[]{:S(2)}, u32[]{:S(2)}) collective-permute-start(f32[2,4,34,1]{3,1,2,0:T(4,128)S(1)} %get-tuple-element.255), channel_id=1, source_target_pairs={{1,0},{3,2},{5,4},{7,6},{9,8},{11,10},{13,12},{15,14},{17,16},{19,... | collective-permute-start | bytes 3272 | tf_op jit(solution)/shard_map/ppermute | solution.py:20
  217.9 4.4 %collective-permute-done.14 = f32[2,4,34,1]{3,1,2,0:T(4,128)S(1)} collective-permute-done((f32[2,4,34,1]{3,1,2,0:T(4,128)S(1)}, f32[2,4,34,1]{3,1,2,0:T(4,128)S(1)}, u32[]{:S(2)}, u32[]{:S(2)}) %collective-permute-start.14) | collective-permute-done | bytes 1120 | tf_op jit(solution)/shard_map/ppermute | solution.py:17
  225.3 4.8 %scatter.91 = f32[2,4,34,130]{3,1,2,0:T(4,128)S(1)} dynamic-update-slice(f32[2,4,34,130]{3,1,2,0:T(4,128)S(1)} %scatter.90, f32[2,4,32,1]{3,1,2,0:T(4,128)S(1)} %slice_select_fusion, s32[]{:T(128)} %constant.509.clone.1, s32[]{:T(128)} %constant.509.clone.1, s32[]{:T(128)} %constant.516.clone.1, s32[]{:T(128)} %constant.522.clone.1) | dynamic-update-slice | bytes 2052 | tf_op jit(solution)/shard_map/scatter | solution.py:44
  230.3 14.4 %all-gather = f32[16,32,128]{2,1,0:T(8,128)S(1)} all-gather(f32[4,32,128]{2,1,0:T(8,128)S(1)} %copy.91), channel_id=2, replica_groups=mesh['mem'=4,'gx'=4,'gy'=2] {'mem'}, dimensions={0}, use_global_device_ids=true | all-gather | bytes 327680 | tf_op jit(solution)/shard_map/all_gather | solution.py:164
  (165 shorter events, 55.0 us)
Async XLA Ops:
  0.6 42.4 %copy-start.6 = (s32[768]{0:T(1024)S(1)}, s32[768]{0:T(1024)}, u32[]{:S(2)}) copy-start(s32[768]{0:T(1024)} %param.60) | copy-start | bytes 9220
  0.7 43.3 %copy-start.3 = (f32[1,2,4,32,128]{4,3,2,1,0:T(8,128)S(1)}, f32[1,2,4,32,128]{4,3,2,1,0:T(8,128)}, u32[]{:S(2)}) copy-start(f32[1,2,4,32,128]{4,3,2,1,0:T(8,128)} %param.54) | copy-start | bytes 393220
  1.5 61.3 %collective-permute-start = (f32[1,4,1,128]{3,1,2,0:T(4,128)S(1)}, f32[1,4,1,128]{3,1,2,0:T(4,128)S(1)}, u32[]{:S(2)}, u32[]{:S(2)}) collective-permute-start(f32[1,4,1,128]{3,1,2,0:T(4,128)S(1)} %copy.117), channel_id=1, source_target_pairs={{0,2},{2,4},{4,6},{1,3},{3,5},{5,7},{8,10},{10,12},{12,14},{9,11},... | collective-permute-start | bytes 6152 | tf_op jit(solution)/shard_map/ppermute | solution.py:17
  3.3 59.6 %collective-permute-start.1 = (f32[1,4,1,128]{3,1,2,0:T(4,128)S(1)}, f32[1,4,1,128]{3,1,2,0:T(4,128)S(1)}, u32[]{:S(2)}, u32[]{:S(2)}) collective-permute-start(f32[1,4,1,128]{3,1,2,0:T(4,128)S(1)} %copy.118), channel_id=1, source_target_pairs={{2,0},{4,2},{6,4},{3,1},{5,3},{7,5},{10,8},{12,10},{14,12},{11,9},... | collective-permute-start | bytes 6152 | tf_op jit(solution)/shard_map/ppermute | solution.py:20
  5.3 62.2 %collective-permute-start.16 = (f32[1,4,1,128]{3,1,2,0:T(4,128)S(1)}, f32[1,4,1,128]{3,1,2,0:T(4,128)S(1)}, u32[]{:S(2)}, u32[]{:S(2)}) collective-permute-start(f32[1,4,1,128]{3,1,2,0:T(4,128)S(1)} %copy.119), channel_id=1, source_target_pairs={{0,2},{2,4},{4,6},{1,3},{3,5},{5,7},{8,10},{10,12},{12,14},{9,11},... | collective-permute-start | bytes 6152 | tf_op jit(solution)/shard_map/ppermute | solution.py:17
  9.7 58.0 %collective-permute-start.17 = (f32[1,4,1,128]{3,1,2,0:T(4,128)S(1)}, f32[1,4,1,128]{3,1,2,0:T(4,128)S(1)}, u32[]{:S(2)}, u32[]{:S(2)}) collective-permute-start(f32[1,4,1,128]{3,1,2,0:T(4,128)S(1)} %copy.120), channel_id=1, source_target_pairs={{2,0},{4,2},{6,4},{3,1},{5,3},{7,5},{10,8},{12,10},{14,12},{11,9},... | collective-permute-start | bytes 6152 | tf_op jit(solution)/shard_map/ppermute | solution.py:20
  17.8 45.0 %copy-start.2 = (f32[1,4,32,128]{3,2,1,0:T(8,128)S(1)}, f32[1,4,32,128]{3,2,1,0:T(8,128)}, u32[]{:S(2)}) copy-start(f32[1,4,32,128]{3,2,1,0:T(8,128)} %param.53) | copy-start | bytes 196612
  17.8 49.8 %copy-start.1 = (f32[1,4,32,128]{3,2,1,0:T(8,128)S(1)}, f32[1,4,32,128]{3,2,1,0:T(8,128)}, u32[]{:S(2)}) copy-start(f32[1,4,32,128]{3,2,1,0:T(8,128)} %param.55) | copy-start | bytes 196612
  63.0 5.2 %collective-permute-start.3 = (f32[1,4,34,1]{3,1,2,0:T(4,128)S(1)}, f32[1,4,34,1]{3,1,2,0:T(4,128)S(1)}, u32[]{:S(2)}, u32[]{:S(2)}) collective-permute-start(f32[1,4,34,1]{3,1,2,0:T(4,128)S(1)} %get-tuple-element.271), channel_id=1, source_target_pairs={{1,0},{3,2},{5,4},{7,6},{9,8},{11,10},{13,12},{15,14},{17,16},{19,... | collective-permute-start | bytes 1640 | tf_op jit(solution)/shard_map/ppermute | solution.py:20
  66.3 6.2 %collective-permute-start.2 = (f32[1,4,34,1]{3,1,2,0:T(4,128)S(1)}, f32[1,4,34,1]{3,1,2,0:T(4,128)S(1)}, u32[]{:S(2)}, u32[]{:S(2)}) collective-permute-start(f32[1,4,34,1]{3,1,2,0:T(4,128)S(1)} %get-tuple-element.270), channel_id=1, source_target_pairs={{0,1},{2,3},{4,5},{6,7},{8,9},{10,11},{12,13},{14,15},{16,17},{18,... | collective-permute-start | bytes 1640 | tf_op jit(solution)/shard_map/ppermute | solution.py:17
  77.8 7.3 %collective-permute-start.5 = (f32[2,4,1,128]{3,1,2,0:T(4,128)S(1)}, f32[2,4,1,128]{3,1,2,0:T(4,128)S(1)}, u32[]{:S(2)}, u32[]{:S(2)}) collective-permute-start(f32[2,4,1,128]{3,1,2,0:T(4,128)S(1)} %get-tuple-element.263), channel_id=1, source_target_pairs={{2,0},{4,2},{6,4},{3,1},{5,3},{7,5},{10,8},{12,10},{14,12},{11,9},... | collective-permute-start | bytes 12296 | tf_op jit(solution)/shard_map/ppermute | solution.py:20
  79.1 6.0 %collective-permute-start.4 = (f32[2,4,1,128]{3,1,2,0:T(4,128)S(1)}, f32[2,4,1,128]{3,1,2,0:T(4,128)S(1)}, u32[]{:S(2)}, u32[]{:S(2)}) collective-permute-start(f32[2,4,1,128]{3,1,2,0:T(4,128)S(1)} %get-tuple-element.262), channel_id=1, source_target_pairs={{0,2},{2,4},{4,6},{1,3},{3,5},{5,7},{8,10},{10,12},{12,14},{9,11},... | collective-permute-start | bytes 12296 | tf_op jit(solution)/shard_map/ppermute | solution.py:17
  82.3 27.3 %collective-permute-start.19 = (f32[1,4,34,1]{3,1,2,0:T(4,128)S(1)}, f32[1,4,34,1]{3,1,2,0:T(4,128)S(1)}, u32[]{:S(2)}, u32[]{:S(2)}) collective-permute-start(f32[1,4,34,1]{3,1,2,0:T(4,128)S(1)} %get-tuple-element.267), channel_id=1, source_target_pairs={{1,0},{3,2},{5,4},{7,6},{9,8},{11,10},{13,12},{15,14},{17,16},{19,... | collective-permute-start | bytes 1640 | tf_op jit(solution)/shard_map/ppermute | solution.py:20
  83.9 25.7 %collective-permute-start.18 = (f32[1,4,34,1]{3,1,2,0:T(4,128)S(1)}, f32[1,4,34,1]{3,1,2,0:T(4,128)S(1)}, u32[]{:S(2)}, u32[]{:S(2)}) collective-permute-start(f32[1,4,34,1]{3,1,2,0:T(4,128)S(1)} %get-tuple-element.266), channel_id=1, source_target_pairs={{0,1},{2,3},{4,5},{6,7},{8,9},{10,11},{12,13},{14,15},{16,17},{18,... | collective-permute-start | bytes 1640 | tf_op jit(solution)/shard_map/ppermute | solution.py:17
  85.4 8.4 %collective-permute-start.7 = (f32[2,4,34,1]{3,1,2,0:T(4,128)S(1)}, f32[2,4,34,1]{3,1,2,0:T(4,128)S(1)}, u32[]{:S(2)}, u32[]{:S(2)}) collective-permute-start(f32[2,4,34,1]{3,1,2,0:T(4,128)S(1)} %get-tuple-element.257), channel_id=1, source_target_pairs={{1,0},{3,2},{5,4},{7,6},{9,8},{11,10},{13,12},{15,14},{17,16},{19,... | collective-permute-start | bytes 3272 | tf_op jit(solution)/shard_map/ppermute | solution.py:20
  89.9 8.3 %collective-permute-start.6 = (f32[2,4,34,1]{3,1,2,0:T(4,128)S(1)}, f32[2,4,34,1]{3,1,2,0:T(4,128)S(1)}, u32[]{:S(2)}, u32[]{:S(2)}) collective-permute-start(f32[2,4,34,1]{3,1,2,0:T(4,128)S(1)} %get-tuple-element.256), channel_id=1, source_target_pairs={{0,1},{2,3},{4,5},{6,7},{8,9},{10,11},{12,13},{14,15},{16,17},{18,... | collective-permute-start | bytes 3272 | tf_op jit(solution)/shard_map/ppermute | solution.py:17
  106.3 3.4 %collective-permute-start.8 = (f32[1,4,1,128]{3,1,2,0:T(4,128)S(1)}, f32[1,4,1,128]{3,1,2,0:T(4,128)S(1)}, u32[]{:S(2)}, u32[]{:S(2)}) collective-permute-start(f32[1,4,1,128]{3,1,2,0:T(4,128)S(1)} %get-tuple-element.274), channel_id=1, source_target_pairs={{0,2},{2,4},{4,6},{1,3},{3,5},{5,7},{8,10},{10,12},{12,14},{9,11},... | collective-permute-start | bytes 6152 | tf_op jit(solution)/shard_map/ppermute | solution.py:17
  108.2 3.4 %collective-permute-start.9 = (f32[1,4,1,128]{3,1,2,0:T(4,128)S(1)}, f32[1,4,1,128]{3,1,2,0:T(4,128)S(1)}, u32[]{:S(2)}, u32[]{:S(2)}) collective-permute-start(f32[1,4,1,128]{3,1,2,0:T(4,128)S(1)} %get-tuple-element.275), channel_id=1, source_target_pairs={{2,0},{4,2},{6,4},{3,1},{5,3},{7,5},{10,8},{12,10},{14,12},{11,9},... | collective-permute-start | bytes 6152 | tf_op jit(solution)/shard_map/ppermute | solution.py:20
  111.7 4.3 %collective-permute-start.11 = (f32[1,4,34,1]{3,1,2,0:T(4,128)S(1)}, f32[1,4,34,1]{3,1,2,0:T(4,128)S(1)}, u32[]{:S(2)}, u32[]{:S(2)}) collective-permute-start(f32[1,4,34,1]{3,1,2,0:T(4,128)S(1)} %get-tuple-element.269), channel_id=1, source_target_pairs={{1,0},{3,2},{5,4},{7,6},{9,8},{11,10},{13,12},{15,14},{17,16},{19,... | collective-permute-start | bytes 1640 | tf_op jit(solution)/shard_map/ppermute | solution.py:20
  113.2 6.2 %collective-permute-start.10 = (f32[1,4,34,1]{3,1,2,0:T(4,128)S(1)}, f32[1,4,34,1]{3,1,2,0:T(4,128)S(1)}, u32[]{:S(2)}, u32[]{:S(2)}) collective-permute-start(f32[1,4,34,1]{3,1,2,0:T(4,128)S(1)} %get-tuple-element.268), channel_id=1, source_target_pairs={{0,1},{2,3},{4,5},{6,7},{8,9},{10,11},{12,13},{14,15},{16,17},{18,... | collective-permute-start | bytes 1640 | tf_op jit(solution)/shard_map/ppermute | solution.py:17
  128.6 82.7 %collective-permute-start.13 = (f32[2,4,1,128]{3,1,2,0:T(4,128)S(1)}, f32[2,4,1,128]{3,1,2,0:T(4,128)S(1)}, u32[]{:S(2)}, u32[]{:S(2)}) collective-permute-start(f32[2,4,1,128]{3,1,2,0:T(4,128)S(1)} %get-tuple-element.261), channel_id=1, source_target_pairs={{2,0},{4,2},{6,4},{3,1},{5,3},{7,5},{10,8},{12,10},{14,12},{11,9},... | collective-permute-start | bytes 12296 | tf_op jit(solution)/shard_map/ppermute | solution.py:20
  129.9 81.4 %collective-permute-start.12 = (f32[2,4,1,128]{3,1,2,0:T(4,128)S(1)}, f32[2,4,1,128]{3,1,2,0:T(4,128)S(1)}, u32[]{:S(2)}, u32[]{:S(2)}) collective-permute-start(f32[2,4,1,128]{3,1,2,0:T(4,128)S(1)} %get-tuple-element.260), channel_id=1, source_target_pairs={{0,2},{2,4},{4,6},{1,3},{3,5},{5,7},{8,10},{10,12},{12,14},{9,11},... | collective-permute-start | bytes 12296 | tf_op jit(solution)/shard_map/ppermute | solution.py:17
  211.5 6.4 %collective-permute-start.15 = (f32[2,4,34,1]{3,1,2,0:T(4,128)S(1)}, f32[2,4,34,1]{3,1,2,0:T(4,128)S(1)}, u32[]{:S(2)}, u32[]{:S(2)}) collective-permute-start(f32[2,4,34,1]{3,1,2,0:T(4,128)S(1)} %get-tuple-element.255), channel_id=1, source_target_pairs={{1,0},{3,2},{5,4},{7,6},{9,8},{11,10},{13,12},{15,14},{17,16},{19,... | collective-permute-start | bytes 3272 | tf_op jit(solution)/shard_map/ppermute | solution.py:20
  215.3 6.9 %collective-permute-start.14 = (f32[2,4,34,1]{3,1,2,0:T(4,128)S(1)}, f32[2,4,34,1]{3,1,2,0:T(4,128)S(1)}, u32[]{:S(2)}, u32[]{:S(2)}) collective-permute-start(f32[2,4,34,1]{3,1,2,0:T(4,128)S(1)} %get-tuple-element.254), channel_id=1, source_target_pairs={{0,1},{2,3},{4,5},{6,7},{8,9},{10,11},{12,13},{14,15},{16,17},{18,... | collective-permute-start | bytes 3272 | tf_op jit(solution)/shard_map/ppermute | solution.py:17
  (3 other events, 61.3 us)
where the time goes:
time: 246 us; the launch traced here: 245 us
  blocking collectives  131 us (53%)
  starting transfers between devices  42.1 us (17%)
  local copies, waits for them, and re-layouts  37.8 us (15%)
  waiting for transfers between devices  22.7 us (9%)
  other arithmetic  5.81 us (2%)
  between operations  3.52 us (1%)
  matrix products  2.68 us (1%)
    psum x1, blocking collectives, body(): rim = lax.psum(rim_part, ('gx', 'gy'))  25 us
    ppermute x10, starting transfers between devices, extended(): lax.ppermute(lax.slice_in_dim(block, 0, width, axis=dim), axis, backward)  21.2 us
    ppermute x10, starting transfers between devices, extended(): lax.ppermute(lax.slice_in_dim(block, block.shape[dim] - width, None, axis...  21 us
    scatter x5, local copies, waits for them, and re-layouts, frame(): padded.at[:, :, 1:1 + size_x, 1 + size_y]  16.9 us
    ppermute x10, waiting for transfers between devices, extended(): lax.ppermute(lax.slice_in_dim(block, block.shape[dim] - width, None, axis...  16.5 us
    all_gather x1, blocking collectives, body(): lax.all_gather(states[5], 'mem', axis=0, tiled=True)  16.5 us
    all_gather x1, blocking collectives, body(): lax.all_gather(states[1], 'mem', axis=0, tiled=True)  16.1 us
    all_gather x1, blocking collectives, body(): lax.all_gather(states[2], 'mem', axis=0, tiled=True)  14.7 us
  transfers between devices with their start and end apart: 20, of which 8 were waited for; matrix products, arithmetic and copies ran while one was open for 9% of the time, Pallas kernels for 0%

commit v1 on v0

--- a/solution.py
+++ b/solution.py
@@ -7,6 +7,18 @@
 ACOUSTIC = 2
 acoustic_substep = 0.2
 drift_step = 0.4
+
+
+def collect(shard, axis, dim):
+    ways, here, hop = (lax.axis_size(axis), lax.axis_index(axis), shard.shape[dim])
+    line, have = (shard, 1)
+    while have < ways:
+        line = jnp.concatenate(
+            [line, lax.ppermute(line, axis, [(d, (d - have) % ways) for d in range(ways)])],
+            axis=dim,
+        )
+        have = 2 * have
+    return jnp.roll(line, here * hop, axis=dim)
 
 
 def extended(block, sides, width):
@@ -164,7 +176,7 @@
         lax.all_gather(states[0], "mem", axis=0, tiled=True),
         lax.all_gather(states[1], "mem", axis=0, tiled=True),
         lax.all_gather(states[2], "mem", axis=0, tiled=True),
-        lax.all_gather(states[3], "mem", axis=0, tiled=True),
+        collect(states[3], "mem", 0),
         lax.all_gather(states[4], "mem", axis=0, tiled=True),
         lax.all_gather(states[5], "mem", axis=0, tiled=True),
     )

time: 246 us -> 242 us (0.984); the launches traced: 245 us -> 237 us
  blocking collectives: 131 us -> 117 us
  starting transfers between devices: 42.1 us -> 44.6 us
    all_gather x1 -> x0, blocking collectives: 13.2 us -> none  [body(): lax.all_gather(states[3], 'mem', axis=0, tiled=True)]
    ppermute x0 -> x2, starting transfers between devices: none -> 2.53 us  [collect(): lax.ppermute(line, axis, [(d, (d - have) % ways) for d in range(ways)])]
  transfers between devices with their start and end apart: 20 -> 22, of which waited for: 8 -> 9; matrix products, arithmetic and copies ran while one was open for 9% -> 13% of each run, Pallas kernels for 0% -> 0%
where the time goes in v1:
time: 242 us; the launch traced here: 237 us
  blocking collectives  117 us (48%)
  starting transfers between devices  44.6 us (18%)
  local copies, waits for them, and re-layouts  38.2 us (16%)
  waiting for transfers between devices  25 us (10%)
  other arithmetic  5.81 us (2%)
  between operations  3.55 us (1%)
  matrix products  2.68 us (1%)
    psum x1, blocking collectives, body(): rim = lax.psum(rim_part, ('gx', 'gy'))  25 us
    ppermute x10, starting transfers between devices, extended(): lax.ppermute(lax.slice_in_dim(block, 0, width, axis=dim), axis, backward)  21.1 us
    ppermute x10, starting transfers between devices, extended(): lax.ppermute(lax.slice_in_dim(block, block.shape[dim] - width, None, axis...  21 us
    scatter x5, local copies, waits for them, and re-layouts, frame(): padded.at[:, :, 1:1 + size_x, 1 + size_y]  16.9 us
    all_gather x1, blocking collectives, body(): lax.all_gather(states[5], 'mem', axis=0, tiled=True)  16.5 us
    ppermute x10, waiting for transfers between devices, extended(): lax.ppermute(lax.slice_in_dim(block, block.shape[dim] - width, None, axis...  16.4 us
    all_gather x1, blocking collectives, body(): lax.all_gather(states[1], 'mem', axis=0, tiled=True)  16.1 us
    all_gather x1, blocking collectives, body(): lax.all_gather(states[2], 'mem', axis=0, tiled=True)  14.7 us
  transfers between devices with their start and end apart: 22, of which 9 were waited for; matrix products, arithmetic and copies ran while one was open for 13% of the time, Pallas kernels for 0%

profile of v1, /device:TPU:10, one launch (start us, length us, event | category | flops | bytes accessed | tf_op | source)
XLA Modules:
  0.0 237.0 jit_solution(13891669978268073537)
XLA Ops:
  5.3 4.3 %collective-permute-start.16 = (f32[1,4,1,128]{3,1,2,0:T(4,128)S(1)}, f32[1,4,1,128]{3,1,2,0:T(4,128)S(1)}, u32[]{:S(2)}, u32[]{:S(2)}) collective-permute-start(f32[1,4,1,128]{3,1,2,0:T(4,128)S(1)} %copy.119), channel_id=1, source_target_pairs={{0,2},{2,4},{4,6},{1,3},{3,5},{5,7},{8,10},{10,12},{12,14},{9,11},... | collective-permute-start | bytes 6152 | tf_op jit(solution)/shard_map/ppermute | solution.py:29
  18.1 25.0 %psum.21 = f32[16,384]{1,0:T(8,128)S(1)} all-reduce(f32[16,384]{1,0:T(8,128)S(1)} %fusion.78), channel_id=1, replica_groups=mesh['mem'=4,'gx'=4,'gy'=2] {'gx','gy'}, use_global_device_ids=true, to_apply=%region_0.0 | all-reduce | flops 6144 | bytes 49152 | tf_op jit(solution)/shard_map/psum | solution.py:94
  44.0 16.5 %all_gather.19 = f32[4,4,4,2048]{3,2,1,0:T(4,128)S(1)} all-gather(f32[1,4,4,2048]{3,2,1,0:T(4,128)S(1)} %get-tuple-element.293), channel_id=1, replica_groups=mesh['mem'=4,'gx'=4,'gy'=2] {'mem'}, dimensions={0}, use_global_device_ids=true | all-gather | bytes 655360 | tf_op jit(solution)/shard_map/all_gather | solution.py:181
  63.0 3.3 %collective-permute-start.3 = (f32[1,4,34,1]{3,1,2,0:T(4,128)S(1)}, f32[1,4,34,1]{3,1,2,0:T(4,128)S(1)}, u32[]{:S(2)}, u32[]{:S(2)}) collective-permute-start(f32[1,4,34,1]{3,1,2,0:T(4,128)S(1)} %get-tuple-element.271), channel_id=1, source_target_pairs={{1,0},{3,2},{5,4},{7,6},{9,8},{11,10},{13,12},{15,14},{17,16},{19,... | collective-permute-start | bytes 1640 | tf_op jit(solution)/shard_map/ppermute | solution.py:32
  68.2 4.3 %collective-permute-done.2 = f32[1,4,34,1]{3,1,2,0:T(4,128)S(1)} collective-permute-done((f32[1,4,34,1]{3,1,2,0:T(4,128)S(1)}, f32[1,4,34,1]{3,1,2,0:T(4,128)S(1)}, u32[]{:S(2)}, u32[]{:S(2)}) %collective-permute-start.2) | collective-permute-done | bytes 576 | tf_op jit(solution)/shard_map/ppermute | solution.py:29
  75.3 2.4 %scatter.71 = f32[4,34,130]{2,0,1:T(4,128)S(1)} dynamic-update-slice(f32[4,34,130]{2,0,1:T(4,128)S(1)} %bitcast.152, f32[4,32,1]{2,0,1:T(4,128)S(1)} %copy.81, s32[]{:T(128)} %constant.540.clone.1, s32[]{:T(128)} %constant.547.clone.1, s32[]{:T(128)} %constant.553.clone.1) | dynamic-update-slice | bytes 1028 | tf_op jit(solution)/shard_map/scatter | solution.py:56
  79.2 3.0 %collective-permute-start.4 = (f32[2,4,1,128]{3,1,2,0:T(4,128)S(1)}, f32[2,4,1,128]{3,1,2,0:T(4,128)S(1)}, u32[]{:S(2)}, u32[]{:S(2)}) collective-permute-start(f32[2,4,1,128]{3,1,2,0:T(4,128)S(1)} %get-tuple-element.262), channel_id=1, source_target_pairs={{0,2},{2,4},{4,6},{1,3},{3,5},{5,7},{8,10},{10,12},{12,14},{9,11},... | collective-permute-start | bytes 12296 | tf_op jit(solution)/shard_map/ppermute | solution.py:29
  85.5 4.6 %collective-permute-start.7 = (f32[2,4,34,1]{3,1,2,0:T(4,128)S(1)}, f32[2,4,34,1]{3,1,2,0:T(4,128)S(1)}, u32[]{:S(2)}, u32[]{:S(2)}) collective-permute-start(f32[2,4,34,1]{3,1,2,0:T(4,128)S(1)} %get-tuple-element.257), channel_id=1, source_target_pairs={{1,0},{3,2},{5,4},{7,6},{9,8},{11,10},{13,12},{15,14},{17,16},{19,... | collective-permute-start | bytes 3272 | tf_op jit(solution)/shard_map/ppermute | solution.py:32
  91.3 2.6 %collective-permute-done.7 = f32[2,4,34,1]{3,1,2,0:T(4,128)S(1)} collective-permute-done((f32[2,4,34,1]{3,1,2,0:T(4,128)S(1)}, f32[2,4,34,1]{3,1,2,0:T(4,128)S(1)}, u32[]{:S(2)}, u32[]{:S(2)}) %collective-permute-start.7) | collective-permute-done | bytes 1120 | tf_op jit(solution)/shard_map/ppermute | solution.py:32
  93.9 4.4 %collective-permute-done.6 = f32[2,4,34,1]{3,1,2,0:T(4,128)S(1)} collective-permute-done((f32[2,4,34,1]{3,1,2,0:T(4,128)S(1)}, f32[2,4,34,1]{3,1,2,0:T(4,128)S(1)}, u32[]{:S(2)}, u32[]{:S(2)}) %collective-permute-start.6) | collective-permute-done | bytes 1120 | tf_op jit(solution)/shard_map/ppermute | solution.py:29
  101.5 4.8 %scatter.79 = f32[2,4,34,130]{3,1,2,0:T(4,128)S(1)} dynamic-update-slice(f32[2,4,34,130]{3,1,2,0:T(4,128)S(1)} %scatter.76, f32[2,4,32,1]{3,1,2,0:T(4,128)S(1)} %slice_select_fusion.2, s32[]{:T(128)} %constant.540.clone.1, s32[]{:T(128)} %constant.540.clone.1, s32[]{:T(128)} %constant.547.clone.1, s32[]{:T(128)} %constant.553.clone.1) | dynamic-update-slice | bytes 2052 | tf_op jit(solution)/shard_map/scatter | solution.py:56
  116.3 3.3 %collective-permute-done.10 = f32[1,4,34,1]{3,1,2,0:T(4,128)S(1)} collective-permute-done((f32[1,4,34,1]{3,1,2,0:T(4,128)S(1)}, f32[1,4,34,1]{3,1,2,0:T(4,128)S(1)}, u32[]{:S(2)}, u32[]{:S(2)}) %collective-permute-start.10) | collective-permute-done | bytes 576 | tf_op jit(solution)/shard_map/ppermute | solution.py:29
  125.9 2.6 %scatter.85 = f32[4,34,130]{2,0,1:T(4,128)S(1)} dynamic-update-slice(f32[4,34,130]{2,0,1:T(4,128)S(1)} %bitcast.151, f32[4,32,1]{2,0,1:T(4,128)S(1)} %copy.88, s32[]{:T(128)} %constant.540.clone.1, s32[]{:T(128)} %constant.547.clone.1, s32[]{:T(128)} %constant.553.clone.1) | dynamic-update-slice | bytes 1028 | tf_op jit(solution)/shard_map/scatter | solution.py:56
  130.1 3.5 %collective-permute-start.12 = (f32[2,4,1,128]{3,1,2,0:T(4,128)S(1)}, f32[2,4,1,128]{3,1,2,0:T(4,128)S(1)}, u32[]{:S(2)}, u32[]{:S(2)}) collective-permute-start(f32[2,4,1,128]{3,1,2,0:T(4,128)S(1)} %get-tuple-element.260), channel_id=1, source_target_pairs={{0,2},{2,4},{4,6},{1,3},{3,5},{5,7},{8,10},{10,12},{12,14},{9,11},... | collective-permute-start | bytes 12296 | tf_op jit(solution)/shard_map/ppermute | solution.py:29
  133.7 16.1 %all-gather.1 = f32[8,4,32,128]{3,2,1,0:T(8,128)S(1)} all-gather(f32[2,4,32,128]{3,2,1,0:T(8,128)S(1)} %copy.92), channel_id=3, replica_groups=mesh['mem'=4,'gx'=4,'gy'=2] {'mem'}, dimensions={0}, use_global_device_ids=true | all-gather | bytes 655360 | tf_op jit(solution)/shard_map/all_gather | solution.py:177
  150.5 14.7 %all-gather.2 = f32[16,32,128]{2,1,0:T(8,128)S(1)} all-gather(f32[4,32,128]{2,1,0:T(8,128)S(1)} %copy.101), channel_id=4, replica_groups=mesh['mem'=4,'gx'=4,'gy'=2] {'mem'}, dimensions={0}, use_global_device_ids=true | all-gather | bytes 327680 | tf_op jit(solution)/shard_map/all_gather | solution.py:178
  166.4 7.0 %psum.22 = f32[4,16,32]{2,1,0:T(8,128)S(1)} all-reduce(f32[4,16,32]{2,1,0:T(8,128)S(1)} %fusion.36), channel_id=1, replica_groups=mesh['mem'=4,'gx'=4,'gy'=2] {'gy'}, use_global_device_ids=true, to_apply=%region_2.3 | all-reduce | flops 2048 | bytes 16384 | tf_op jit(solution)/shard_map/psum | solution.py:163
  173.4 10.3 %psum.23 = f32[4,16,32]{2,1,0:T(8,128)S(1)} all-reduce(f32[4,16,32]{2,1,0:T(8,128)S(1)} %psum.22), channel_id=1, replica_groups=mesh['mem'=4,'gx'=4,'gy'=2] {'gx'}, use_global_device_ids=true, to_apply=%region_3.4 | all-reduce | flops 2048 | bytes 16384 | tf_op jit(solution)/shard_map/psum | solution.py:164
  183.7 13.4 %all-gather.3 = f32[16,16,32]{2,1,0:T(8,128)S(1)} all-gather(f32[4,16,32]{2,1,0:T(8,128)S(1)} %broadcast_divide_fusion), channel_id=5, replica_groups=mesh['mem'=4,'gx'=4,'gy'=2] {'mem'}, dimensions={0}, use_global_device_ids=true | all-gather | bytes 40960 | tf_op jit(solution)/shard_map/all_gather | solution.py:180
  197.9 3.7 %collective-permute-start.15 = (f32[2,4,34,1]{3,1,2,0:T(4,128)S(1)}, f32[2,4,34,1]{3,1,2,0:T(4,128)S(1)}, u32[]{:S(2)}, u32[]{:S(2)}) collective-permute-start(f32[2,4,34,1]{3,1,2,0:T(4,128)S(1)} %get-tuple-element.255), channel_id=1, source_target_pairs={{1,0},{3,2},{5,4},{7,6},{9,8},{11,10},{13,12},{15,14},{17,16},{19,... | collective-permute-start | bytes 3272 | tf_op jit(solution)/shard_map/ppermute | solution.py:32
  204.2 4.4 %collective-permute-done.14 = f32[2,4,34,1]{3,1,2,0:T(4,128)S(1)} collective-permute-done((f32[2,4,34,1]{3,1,2,0:T(4,128)S(1)}, f32[2,4,34,1]{3,1,2,0:T(4,128)S(1)}, u32[]{:S(2)}, u32[]{:S(2)}) %collective-permute-start.14) | collective-permute-done | bytes 1120 | tf_op jit(solution)/shard_map/ppermute | solution.py:29
  211.7 4.8 %scatter.91 = f32[2,4,34,130]{3,1,2,0:T(4,128)S(1)} dynamic-update-slice(f32[2,4,34,130]{3,1,2,0:T(4,128)S(1)} %scatter.90, f32[2,4,32,1]{3,1,2,0:T(4,128)S(1)} %slice_select_fusion, s32[]{:T(128)} %constant.540.clone.1, s32[]{:T(128)} %constant.540.clone.1, s32[]{:T(128)} %constant.547.clone.1, s32[]{:T(128)} %constant.553.clone.1) | dynamic-update-slice | bytes 2052 | tf_op jit(solution)/shard_map/scatter | solution.py:56
  216.7 14.2 %all-gather = f32[16,32,128]{2,1,0:T(8,128)S(1)} all-gather(f32[4,32,128]{2,1,0:T(8,128)S(1)} %copy.91), channel_id=2, replica_groups=mesh['mem'=4,'gx'=4,'gy'=2] {'mem'}, dimensions={0}, use_global_device_ids=true | all-gather | bytes 327680 | tf_op jit(solution)/shard_map/all_gather | solution.py:176
  231.6 2.5 %collective-permute-start.21 = (f32[2,32,128]{2,1,0:T(8,128)S(1)}, f32[2,32,128]{2,1,0:T(8,128)S(1)}, u32[]{:S(2)}, u32[]{:S(2)}) collective-permute-start(f32[2,32,128]{2,1,0:T(8,128)S(1)} %pad_maximum_fusion.9), channel_id=1, source_target_pairs={{0,16},{8,24},{16,0},{24,8},{1,17},{9,25},{17,1},{25,9},{2,18},{10... | collective-permute-start | bytes 98312 | tf_op jit(solution)/shard_map/ppermute | solution.py:17
  (175 shorter events, 57.9 us)
Async XLA Ops:
  1.5 61.3 %collective-permute-start = (f32[1,4,1,128]{3,1,2,0:T(4,128)S(1)}, f32[1,4,1,128]{3,1,2,0:T(4,128)S(1)}, u32[]{:S(2)}, u32[]{:S(2)}) collective-permute-start(f32[1,4,1,128]{3,1,2,0:T(4,128)S(1)} %copy.117), channel_id=1, source_target_pairs={{0,2},{2,4},{4,6},{1,3},{3,5},{5,7},{8,10},{10,12},{12,14},{9,11},... | collective-permute-start | bytes 6152 | tf_op jit(solution)/shard_map/ppermute | solution.py:29
  3.3 59.6 %collective-permute-start.1 = (f32[1,4,1,128]{3,1,2,0:T(4,128)S(1)}, f32[1,4,1,128]{3,1,2,0:T(4,128)S(1)}, u32[]{:S(2)}, u32[]{:S(2)}) collective-permute-start(f32[1,4,1,128]{3,1,2,0:T(4,128)S(1)} %copy.118), channel_id=1, source_target_pairs={{2,0},{4,2},{6,4},{3,1},{5,3},{7,5},{10,8},{12,10},{14,12},{11,9},... | collective-permute-start | bytes 6152 | tf_op jit(solution)/shard_map/ppermute | solution.py:32
  5.3 62.3 %collective-permute-start.16 = (f32[1,4,1,128]{3,1,2,0:T(4,128)S(1)}, f32[1,4,1,128]{3,1,2,0:T(4,128)S(1)}, u32[]{:S(2)}, u32[]{:S(2)}) collective-permute-start(f32[1,4,1,128]{3,1,2,0:T(4,128)S(1)} %copy.119), channel_id=1, source_target_pairs={{0,2},{2,4},{4,6},{1,3},{3,5},{5,7},{8,10},{10,12},{12,14},{9,11},... | collective-permute-start | bytes 6152 | tf_op jit(solution)/shard_map/ppermute | solution.py:29
  9.7 58.0 %collective-permute-start.17 = (f32[1,4,1,128]{3,1,2,0:T(4,128)S(1)}, f32[1,4,1,128]{3,1,2,0:T(4,128)S(1)}, u32[]{:S(2)}, u32[]{:S(2)}) collective-permute-start(f32[1,4,1,128]{3,1,2,0:T(4,128)S(1)} %copy.120), channel_id=1, source_target_pairs={{2,0},{4,2},{6,4},{3,1},{5,3},{7,5},{10,8},{12,10},{14,12},{11,9},... | collective-permute-start | bytes 6152 | tf_op jit(solution)/shard_map/ppermute | solution.py:32
  17.8 45.1 %copy-start.2 = (f32[1,4,32,128]{3,2,1,0:T(8,128)S(1)}, f32[1,4,32,128]{3,2,1,0:T(8,128)}, u32[]{:S(2)}) copy-start(f32[1,4,32,128]{3,2,1,0:T(8,128)} %param.53) | copy-start | bytes 196612
  17.8 49.8 %copy-start.1 = (f32[1,4,32,128]{3,2,1,0:T(8,128)S(1)}, f32[1,4,32,128]{3,2,1,0:T(8,128)}, u32[]{:S(2)}) copy-start(f32[1,4,32,128]{3,2,1,0:T(8,128)} %param.55) | copy-start | bytes 196612
  63.0 5.2 %collective-permute-start.3 = (f32[1,4,34,1]{3,1,2,0:T(4,128)S(1)}, f32[1,4,34,1]{3,1,2,0:T(4,128)S(1)}, u32[]{:S(2)}, u32[]{:S(2)}) collective-permute-start(f32[1,4,34,1]{3,1,2,0:T(4,128)S(1)} %get-tuple-element.271), channel_id=1, source_target_pairs={{1,0},{3,2},{5,4},{7,6},{9,8},{11,10},{13,12},{15,14},{17,16},{19,... | collective-permute-start | bytes 1640 | tf_op jit(solution)/shard_map/ppermute | solution.py:32
  66.3 6.2 %collective-permute-start.2 = (f32[1,4,34,1]{3,1,2,0:T(4,128)S(1)}, f32[1,4,34,1]{3,1,2,0:T(4,128)S(1)}, u32[]{:S(2)}, u32[]{:S(2)}) collective-permute-start(f32[1,4,34,1]{3,1,2,0:T(4,128)S(1)} %get-tuple-element.270), channel_id=1, source_target_pairs={{0,1},{2,3},{4,5},{6,7},{8,9},{10,11},{12,13},{14,15},{16,17},{18,... | collective-permute-start | bytes 1640 | tf_op jit(solution)/shard_map/ppermute | solution.py:29
  77.9 7.3 %collective-permute-start.5 = (f32[2,4,1,128]{3,1,2,0:T(4,128)S(1)}, f32[2,4,1,128]{3,1,2,0:T(4,128)S(1)}, u32[]{:S(2)}, u32[]{:S(2)}) collective-permute-start(f32[2,4,1,128]{3,1,2,0:T(4,128)S(1)} %get-tuple-element.263), channel_id=1, source_target_pairs={{2,0},{4,2},{6,4},{3,1},{5,3},{7,5},{10,8},{12,10},{14,12},{11,9},... | collective-permute-start | bytes 12296 | tf_op jit(solution)/shard_map/ppermute | solution.py:32
  79.2 6.0 %collective-permute-start.4 = (f32[2,4,1,128]{3,1,2,0:T(4,128)S(1)}, f32[2,4,1,128]{3,1,2,0:T(4,128)S(1)}, u32[]{:S(2)}, u32[]{:S(2)}) collective-permute-start(f32[2,4,1,128]{3,1,2,0:T(4,128)S(1)} %get-tuple-element.262), channel_id=1, source_target_pairs={{0,2},{2,4},{4,6},{1,3},{3,5},{5,7},{8,10},{10,12},{12,14},{9,11},... | collective-permute-start | bytes 12296 | tf_op jit(solution)/shard_map/ppermute | solution.py:29
  82.4 27.3 %collective-permute-start.19 = (f32[1,4,34,1]{3,1,2,0:T(4,128)S(1)}, f32[1,4,34,1]{3,1,2,0:T(4,128)S(1)}, u32[]{:S(2)}, u32[]{:S(2)}) collective-permute-start(f32[1,4,34,1]{3,1,2,0:T(4,128)S(1)} %get-tuple-element.267), channel_id=1, source_target_pairs={{1,0},{3,2},{5,4},{7,6},{9,8},{11,10},{13,12},{15,14},{17,16},{19,... | collective-permute-start | bytes 1640 | tf_op jit(solution)/shard_map/ppermute | solution.py:32
  84.0 25.8 %collective-permute-start.18 = (f32[1,4,34,1]{3,1,2,0:T(4,128)S(1)}, f32[1,4,34,1]{3,1,2,0:T(4,128)S(1)}, u32[]{:S(2)}, u32[]{:S(2)}) collective-permute-start(f32[1,4,34,1]{3,1,2,0:T(4,128)S(1)} %get-tuple-element.266), channel_id=1, source_target_pairs={{0,1},{2,3},{4,5},{6,7},{8,9},{10,11},{12,13},{14,15},{16,17},{18,... | collective-permute-start | bytes 1640 | tf_op jit(solution)/shard_map/ppermute | solution.py:29
  85.5 8.4 %collective-permute-start.7 = (f32[2,4,34,1]{3,1,2,0:T(4,128)S(1)}, f32[2,4,34,1]{3,1,2,0:T(4,128)S(1)}, u32[]{:S(2)}, u32[]{:S(2)}) collective-permute-start(f32[2,4,34,1]{3,1,2,0:T(4,128)S(1)} %get-tuple-element.257), channel_id=1, source_target_pairs={{1,0},{3,2},{5,4},{7,6},{9,8},{11,10},{13,12},{15,14},{17,16},{19,... | collective-permute-start | bytes 3272 | tf_op jit(solution)/shard_map/ppermute | solution.py:32
  90.0 8.3 %collective-permute-start.6 = (f32[2,4,34,1]{3,1,2,0:T(4,128)S(1)}, f32[2,4,34,1]{3,1,2,0:T(4,128)S(1)}, u32[]{:S(2)}, u32[]{:S(2)}) collective-permute-start(f32[2,4,34,1]{3,1,2,0:T(4,128)S(1)} %get-tuple-element.256), channel_id=1, source_target_pairs={{0,1},{2,3},{4,5},{6,7},{8,9},{10,11},{12,13},{14,15},{16,17},{18,... | collective-permute-start | bytes 3272 | tf_op jit(solution)/shard_map/ppermute | solution.py:29
  106.5 3.4 %collective-permute-start.8 = (f32[1,4,1,128]{3,1,2,0:T(4,128)S(1)}, f32[1,4,1,128]{3,1,2,0:T(4,128)S(1)}, u32[]{:S(2)}, u32[]{:S(2)}) collective-permute-start(f32[1,4,1,128]{3,1,2,0:T(4,128)S(1)} %get-tuple-element.274), channel_id=1, source_target_pairs={{0,2},{2,4},{4,6},{1,3},{3,5},{5,7},{8,10},{10,12},{12,14},{9,11},... | collective-permute-start | bytes 6152 | tf_op jit(solution)/shard_map/ppermute | solution.py:29
  108.4 3.4 %collective-permute-start.9 = (f32[1,4,1,128]{3,1,2,0:T(4,128)S(1)}, f32[1,4,1,128]{3,1,2,0:T(4,128)S(1)}, u32[]{:S(2)}, u32[]{:S(2)}) collective-permute-start(f32[1,4,1,128]{3,1,2,0:T(4,128)S(1)} %get-tuple-element.275), channel_id=1, source_target_pairs={{2,0},{4,2},{6,4},{3,1},{5,3},{7,5},{10,8},{12,10},{14,12},{11,9},... | collective-permute-start | bytes 6152 | tf_op jit(solution)/shard_map/ppermute | solution.py:32
  111.9 4.4 %collective-permute-start.11 = (f32[1,4,34,1]{3,1,2,0:T(4,128)S(1)}, f32[1,4,34,1]{3,1,2,0:T(4,128)S(1)}, u32[]{:S(2)}, u32[]{:S(2)}) collective-permute-start(f32[1,4,34,1]{3,1,2,0:T(4,128)S(1)} %get-tuple-element.269), channel_id=1, source_target_pairs={{1,0},{3,2},{5,4},{7,6},{9,8},{11,10},{13,12},{15,14},{17,16},{19,... | collective-permute-start | bytes 1640 | tf_op jit(solution)/shard_map/ppermute | solution.py:32
  113.4 6.2 %collective-permute-start.10 = (f32[1,4,34,1]{3,1,2,0:T(4,128)S(1)}, f32[1,4,34,1]{3,1,2,0:T(4,128)S(1)}, u32[]{:S(2)}, u32[]{:S(2)}) collective-permute-start(f32[1,4,34,1]{3,1,2,0:T(4,128)S(1)} %get-tuple-element.268), channel_id=1, source_target_pairs={{0,1},{2,3},{4,5},{6,7},{8,9},{10,11},{12,13},{14,15},{16,17},{18,... | collective-permute-start | bytes 1640 | tf_op jit(solution)/shard_map/ppermute | solution.py:29
  128.8 68.9 %collective-permute-start.13 = (f32[2,4,1,128]{3,1,2,0:T(4,128)S(1)}, f32[2,4,1,128]{3,1,2,0:T(4,128)S(1)}, u32[]{:S(2)}, u32[]{:S(2)}) collective-permute-start(f32[2,4,1,128]{3,1,2,0:T(4,128)S(1)} %get-tuple-element.261), channel_id=1, source_target_pairs={{2,0},{4,2},{6,4},{3,1},{5,3},{7,5},{10,8},{12,10},{14,12},{11,9},... | collective-permute-start | bytes 12296 | tf_op jit(solution)/shard_map/ppermute | solution.py:32
  130.1 67.6 %collective-permute-start.12 = (f32[2,4,1,128]{3,1,2,0:T(4,128)S(1)}, f32[2,4,1,128]{3,1,2,0:T(4,128)S(1)}, u32[]{:S(2)}, u32[]{:S(2)}) collective-permute-start(f32[2,4,1,128]{3,1,2,0:T(4,128)S(1)} %get-tuple-element.260), channel_id=1, source_target_pairs={{0,2},{2,4},{4,6},{1,3},{3,5},{5,7},{8,10},{10,12},{12,14},{9,11},... | collective-permute-start | bytes 12296 | tf_op jit(solution)/shard_map/ppermute | solution.py:29
  165.9 65.6 %collective-permute-start.20 = (f32[1,32,128]{2,1,0:T(8,128)S(1)}, f32[1,32,128]{2,1,0:T(8,128)S(1)}, u32[]{:S(2)}, u32[]{:S(2)}) collective-permute-start(f32[1,32,128]{2,1,0:T(8,128)S(1)} %bitcast.165), channel_id=1, source_target_pairs={{0,24},{8,0},{16,8},{24,16},{1,25},{9,1},{17,9},{25,17},{2,26},{10... | collective-permute-start | bytes 49160 | tf_op jit(solution)/shard_map/ppermute | solution.py:17
  197.9 6.3 %collective-permute-start.15 = (f32[2,4,34,1]{3,1,2,0:T(4,128)S(1)}, f32[2,4,34,1]{3,1,2,0:T(4,128)S(1)}, u32[]{:S(2)}, u32[]{:S(2)}) collective-permute-start(f32[2,4,34,1]{3,1,2,0:T(4,128)S(1)} %get-tuple-element.255), channel_id=1, source_target_pairs={{1,0},{3,2},{5,4},{7,6},{9,8},{11,10},{13,12},{15,14},{17,16},{19,... | collective-permute-start | bytes 3272 | tf_op jit(solution)/shard_map/ppermute | solution.py:32
  201.6 6.9 %collective-permute-start.14 = (f32[2,4,34,1]{3,1,2,0:T(4,128)S(1)}, f32[2,4,34,1]{3,1,2,0:T(4,128)S(1)}, u32[]{:S(2)}, u32[]{:S(2)}) collective-permute-start(f32[2,4,34,1]{3,1,2,0:T(4,128)S(1)} %get-tuple-element.254), channel_id=1, source_target_pairs={{0,1},{2,3},{4,5},{6,7},{8,9},{10,11},{12,13},{14,15},{16,17},{18,... | collective-permute-start | bytes 3272 | tf_op jit(solution)/shard_map/ppermute | solution.py:29
  231.6 4.8 %collective-permute-start.21 = (f32[2,32,128]{2,1,0:T(8,128)S(1)}, f32[2,32,128]{2,1,0:T(8,128)S(1)}, u32[]{:S(2)}, u32[]{:S(2)}) collective-permute-start(f32[2,32,128]{2,1,0:T(8,128)S(1)} %pad_maximum_fusion.9), channel_id=1, source_target_pairs={{0,16},{8,24},{16,0},{24,8},{1,17},{9,25},{17,1},{25,9},{2,18},{10... | collective-permute-start | bytes 98312 | tf_op jit(solution)/shard_map/ppermute | solution.py:17
  (5 other events, 147.2 us)
